TPU v7x, 512 devices: a whole 4x8x8 slice. The times are simulated.
512 devices in a mesh: dp: 32 (over y, x), seq: 16 (over z, core).
Axes of the slice: x: 4, y: 8, z: 8, core: 2. Of those that a mesh axis runs over, the one named last changes fastest.
Arguments:
- queries: bfloat16 [32, 2048, 2048], P('dp', 'seq'), may hold values from -6 to 6
- keys_in: bfloat16 [32, 2048, 2048], P('dp', 'seq'), may hold values from -6 to 6
- values_in: bfloat16 [32, 2048, 2048], P('dp', 'seq'), may hold values from -6 to 6
- grad_out: bfloat16 [32, 2048, 2048], P('dp', 'seq'), may hold values from -6 to 6
- feat_w: bfloat16 [2, 16, 128, 128], replicated, may hold values from -0.5 to 0.5
Outputs:
- grad_queries: bfloat16 [32, 2048, 2048], P('dp', 'seq')
- grad_keys: bfloat16 [32, 2048, 2048], P('dp', 'seq')
- grad_values: bfloat16 [32, 2048, 2048], P('dp', 'seq')
- grad_feat: float32 [4096, 128], P('dp')
All inputs are finite; a program needn't handle non-finite values.
Results may differ from a plain program's by a relative error of at most 0.0064.
Values sent between devices are 32-bit elements; how exact they have to be, the bound alone decides.
A program may use at most 128 MiB of HBM per device.

v0:
```python
import math
import jax
import jax.numpy as jnp
from jax import lax
from jax.sharding import PartitionSpec as P


def carried_in(value, axis, join, neutral, backward):
    count, mine = (lax.axis_size(axis), lax.axis_index(axis))
    pieces = lax.all_gather(value, axis)
    if backward:
        pieces = pieces[::-1]
        mine = count - 1 - mine
    running = jnp.full_like(value, 0) + jnp.asarray(neutral, value.dtype)

    def lap(position, running):
        longer = join(running, pieces[position])
        return jnp.where(position < mine, longer, running)

    return lax.fori_loop(0, count - 1, lap, running)


def add_one(earlier, later):
    return earlier + later


def body(queries, keys_in, values_in, grad_out, feat_w):
    seq_count = lax.axis_size("seq")
    rep_count = lax.axis_size("dp")
    rows = queries.shape[1]
    heads = feat_w.shape[1]
    hsize = feat_w.shape[2]
    scale = 1.0 / math.sqrt(hsize * rows * seq_count)
    gscale = 1.0 / math.sqrt(rows * seq_count * rep_count)
    shape = (rows, heads, hsize)
    q_heads = queries[0].reshape(shape)
    k_heads = keys_in[0].reshape(shape)
    v_heads = values_in[0].reshape(shape)
    g_heads = grad_out[0].reshape(shape)
    f32 = jnp.float32
    bf16 = jnp.bfloat16
    feat_q = jnp.einsum("tha,hab->thb", q_heads, feat_w[0], preferred_element_type=f32).astype(bf16)
    feat_k = jnp.einsum("tha,hab->thb", k_heads, feat_w[1], preferred_element_type=f32).astype(bf16)
    sterm = jnp.einsum("tha,thb->hab", feat_k, v_heads, preferred_element_type=f32)
    gterm = jnp.einsum("tha,thb->hab", feat_q, g_heads, preferred_element_type=f32)
    zeros = jnp.zeros(sterm.shape, f32)
    prefix = carried_in(sterm, "seq", add_one, zeros, False)
    suffix = carried_in(gterm, "seq", add_one, zeros, True)
    causal = jnp.tril(jnp.ones((rows, rows), dtype=bool))
    p_mat = jnp.where(
        causal, scale * jnp.einsum("tha,sha->hts", feat_q, feat_k, preferred_element_type=f32), 0.0
    ).astype(bf16)
    q_mat = jnp.where(
        causal,
        scale * jnp.einsum("tha,sha->hts", g_heads, v_heads, preferred_element_type=f32),
        0.0,
    ).astype(bf16)
    state_b = prefix.astype(bf16)
    grad_b = suffix.astype(bf16)
    d_featq = (
        scale * jnp.einsum("thb,hab->tha", g_heads, state_b, preferred_element_type=f32)
        + jnp.einsum("hts,sha->tha", q_mat, feat_k, preferred_element_type=f32)
    ).astype(bf16)
    d_featk = (
        scale * jnp.einsum("thb,hab->tha", v_heads, grad_b, preferred_element_type=f32)
        + jnp.einsum("hts,tha->sha", q_mat, feat_q, preferred_element_type=f32)
    ).astype(bf16)
    d_values = (
        scale * jnp.einsum("tha,hab->thb", feat_k, grad_b, preferred_element_type=f32)
        + jnp.einsum("hts,thb->shb", p_mat, g_heads, preferred_element_type=f32)
    ).astype(bf16)
    d_queries = jnp.einsum("thb,hab->tha", d_featq, feat_w[0], preferred_element_type=f32).astype(
        bf16
    )
    d_keys = jnp.einsum("thb,hab->tha", d_featk, feat_w[1], preferred_element_type=f32).astype(bf16)
    wgrad_q = jnp.einsum("tha,thb->hab", q_heads, d_featq, preferred_element_type=f32)
    wgrad_k = jnp.einsum("tha,thb->hab", k_heads, d_featk, preferred_element_type=f32)
    local_grad = jnp.stack([wgrad_q, wgrad_k]).reshape(2 * heads * hsize, hsize)
    seq_total = lax.psum(local_grad, "seq")
    owned = lax.psum_scatter(seq_total, "dp", scatter_dimension=0, tiled=True)
    flat = (1, rows, heads * hsize)
    return (d_queries.reshape(flat), d_keys.reshape(flat), d_values.reshape(flat), owned * gscale)


def solution(mesh):
    return jax.shard_map(
        body,
        mesh=mesh,
        in_specs=(
            P("dp", "seq", None),
            P("dp", "seq", None),
            P("dp", "seq", None),
            P("dp", "seq", None),
            P(),
        ),
        out_specs=(P("dp", "seq", None), P("dp", "seq", None), P("dp", "seq", None), P("dp", None)),
        check_vma=False,
    )
```

profile of v0, /device:TPU:1, one launch (start us, length us, event | category | flops | bytes accessed | tf_op | source)
XLA Modules:
  0.0 593.4 jit_solution(17331871863249463423)
XLA Ops:
  18.7 2.4 fusion.5
  21.1 96.6 %all-gather.5.cloned.1.call-done = f32[256,128,128]{2,1,0:T(8,128)} async-done(((f32[16,128,128]{2,1,0:T(8,128)}), f32[256,128,128]{2,1,0:T(8,128)}) %all-gather.5.cloned.1.call-update) | async-done | bytes 16777232 | tf_op jit(solution)/shard_map/all_gather | solution.py:10
  117.7 24.4 %while.28 = (s32[]{:T(128)}, f32[16,128,128]{2,1,0:T(8,128)S(1)}, s32[]{:T(128)}, f32[16,16,128,128]{3,2,1,0:T(8,128)}, s32[]{:T(128)}, /*index=5*/s32[]{:T(128)}) while((s32[]{:T(128)}, f32[16,128,128]{2,1,0:T(8,128)S(1)}, s32[]{:T(128)}, f32[16,16,128,128]{3,2,1,0:T(8,128)}, s32[]{:T(128)}, /*index=5*/s32[]{:T(128)}) %tuple.79), condition=%wide.region_1.2_spmd.clone, body=%wide.region_0.1_spmd.clone.sunk | while | flops 786436 | bytes 3145821 | solution.py:20
  119.3 1.6 add_select_fusion.4
  122.6 1.6 add_select_fusion.4
  125.8 1.6 add_select_fusion.4
  129.0 1.6 add_select_fusion.4
  130.6 1.7 add_select_fusion.4
  134.0 1.6 add_select_fusion.4
  137.2 1.6 add_select_fusion.4
  138.8 1.7 add_select_fusion.4
  140.5 1.6 add_select_fusion.4
  144.0 2.5 convolution_bitcast_fusion.2
  146.5 70.1 %all-gather.7.cloned.1.call-done = f32[256,128,128]{2,1,0:T(8,128)} async-done(((f32[16,128,128]{2,1,0:T(8,128)}), f32[256,128,128]{2,1,0:T(8,128)}) %all-gather.7.cloned.1.call-update) | async-done | bytes 16777232 | tf_op jit(solution)/shard_map/all_gather | solution.py:10
  216.6 11.6 %rev.3 = f32[16,16,128,128]{3,2,1,0:T(8,128)} reverse(f32[16,16,128,128]{3,2,1,0:T(8,128)} %bitcast.81), dimensions={0} | reverse | bytes 33554432 | tf_op jit(solution)/shard_map/rev | solution.py:12
  228.3 24.2 %while.29 = (s32[]{:T(128)}, f32[16,128,128]{2,1,0:T(8,128)S(1)}, s32[]{:T(128)}, f32[16,16,128,128]{3,2,1,0:T(8,128)}, s32[]{:T(128)}, /*index=5*/s32[]{:T(128)}) while((s32[]{:T(128)}, f32[16,128,128]{2,1,0:T(8,128)S(1)}, s32[]{:T(128)}, f32[16,16,128,128]{3,2,1,0:T(8,128)}, s32[]{:T(128)}, /*index=5*/s32[]{:T(128)}) %tuple.68), condition=%wide.region_3.4_spmd.clone, body=%wide.region_2.3_spmd.clone.sunk | while | flops 786436 | bytes 3145821 | solution.py:20
  228.3 1.6 add_select_fusion.5
  229.9 1.6 add_select_fusion.5
  231.6 1.6 add_select_fusion.5
  233.2 1.6 add_select_fusion.5
  234.8 1.6 add_select_fusion.5
  238.0 1.6 add_select_fusion.5
  239.6 1.6 add_select_fusion.5
  241.2 1.6 add_select_fusion.5
  246.1 1.6 add_select_fusion.5
  247.7 1.6 add_select_fusion.5
  257.7 2.8 pad_maximum_fusion
  260.6 2.1 convolution_convert_fusion.1
  264.0 1.7 fusion.8
  265.7 208.6 %reduce-scatter.2.cloned.1.call-done = f32[128,128]{1,0:T(8,128)} async-done(((f32[4096,128]{1,0:T(8,128)}), f32[128,128]{1,0:T(8,128)}) %reduce-scatter.2.cloned.1.call-update) | async-done | bytes 65552 | tf_op jit(solution)/shard_map/reduce_scatter | solution.py:80
  476.9 2.0 copy.52
  479.9 105.5 %all-reduce.2.cloned.1.call-done = f32[128,128]{1,0:T(8,128)} async-done(((f32[128,128]{1,0:T(8,128)}), f32[128,128]{1,0:T(8,128)}) %all-reduce.2.cloned.1.call-update) | async-done | bytes 65552 | tf_op jit(solution)/shard_map/psum | solution.py:79
  (52 shorter events, 42.3 us)
Async XLA Ops:
  7.2 110.5 %all-gather.5.cloned.1.call-start = ((), (), s32[]{:S(2)}) async-start(), calls=%async_computation.1 | async-start | bytes 17825792 | tf_op jit(solution)/shard_map/all_gather | solution.py:10
  8.5 4.3 copy-start.3
  9.9 5.6 copy-start.4
  12.8 203.8 %all-gather.7.cloned.1.call-start = ((), (), s32[]{:S(2)}) async-start(), calls=%async_computation.2 | async-start | bytes 17825792 | tf_op jit(solution)/shard_map/all_gather | solution.py:10
  15.5 3.2 copy-start.5
  17.1 1.6 copy-start
  18.6 455.7 %reduce-scatter.2.cloned.1.call-start = ((), (), s32[]{:S(2)}) async-start(), calls=%async_computation.3 | async-start | bytes 2162688 | tf_op jit(solution)/shard_map/reduce_scatter | solution.py:80
  228.3 25.8 %copy-start.1 = (bf16[128,16,128]{0,2,1:T(8,128)(2,1)S(1)}, bf16[128,16,128]{0,2,1:T(8,128)(2,1)}, u32[]{:S(2)}) copy-start(bf16[128,16,128]{0,2,1:T(8,128)(2,1)} %copy-done) | copy-start | bytes 1572868
  255.4 0.8 copy-start.2
  260.5 324.9 %all-reduce.2.cloned.1.call-start = ((), (), s32[]{:S(2)}) async-start(), calls=%async_computation.4 | async-start | bytes 131072 | tf_op jit(solution)/shard_map/psum | solution.py:79
Sparse Core Ops, SparseCore 0:
  12.9 104.7 all-gather.4
  119.8 96.7 all-gather.6
  260.6 213.6 reduce-scatter.1
  476.6 108.7 all-reduce.1
where the time goes:
time: 595 us; the launch traced here: 593 us
  waiting for transfers between devices  481 us (81%)
  other arithmetic  52.2 us (9%)
  matrix products  23.7 us (4%)
  local copies, waits for them, and re-layouts  21.8 us (4%)
  between operations  14 us (2%)
    reduce_scatter x1, waiting for transfers between devices, body(): owned = lax.psum_scatter(seq_total, 'dp', scatter_dimension=0, tiled=True)  209 us
    all_gather x2, waiting for transfers between devices, carried_in(): pieces = lax.all_gather(value, axis)  167 us
    psum x1, waiting for transfers between devices, body(): seq_total = lax.psum(local_grad, 'seq')  105 us
    select_n x30, other arithmetic, lap(): return jnp.where(position < mine, longer, running)  48 us
  transfers between devices with their start and end apart: 4, of which 4 were waited for; matrix products, arithmetic and copies ran while one was open for 8% of the time, Pallas kernels for 0%

commit v1 on v0

--- a/solution.py
+++ b/solution.py
@@ -76,7 +76,7 @@
     wgrad_q = jnp.einsum("tha,thb->hab", q_heads, d_featq, preferred_element_type=f32)
     wgrad_k = jnp.einsum("tha,thb->hab", k_heads, d_featk, preferred_element_type=f32)
     local_grad = jnp.stack([wgrad_q, wgrad_k]).reshape(2 * heads * hsize, hsize)
-    seq_total = lax.psum(local_grad, "seq")
+    seq_total = jnp.sum(lax.all_gather(local_grad, "seq"), axis=0)
     owned = lax.psum_scatter(seq_total, "dp", scatter_dimension=0, tiled=True)
     flat = (1, rows, heads * hsize)
     return (d_queries.reshape(flat), d_keys.reshape(flat), d_values.reshape(flat), owned * gscale)

time: 595 us -> 678 us (1.14)
  waiting for transfers between devices: 481 us -> 548 us
  other arithmetic: 52.2 us -> 65.3 us
    all_gather x0 -> x1, waiting for transfers between devices: none -> 176 us  [body(): seq_total = jnp.sum(lax.all_gather(local_grad, 'seq'), axis=0)]
    psum x1 -> x0, waiting for transfers between devices: 105 us -> none  [body(): seq_total = lax.psum(local_grad, 'seq')]
    reduce_sum x0 -> x1, other arithmetic: none -> 13.1 us  [body(): seq_total = jnp.sum(lax.all_gather(local_grad, 'seq'), axis=0)]
  transfers between devices with their start and end apart: 4 -> 4, of which waited for: 4 -> 4; matrix products, arithmetic and copies ran while one was open for 8% -> 7% of each run, Pallas kernels for 0% -> 0%
where the time goes in v1:
time: 678 us; the launch traced here: 672 us
  waiting for transfers between devices  548 us (81%)
  other arithmetic  65.3 us (10%)
  matrix products  22.9 us (3%)
  local copies, waits for them, and re-layouts  20.7 us (3%)
  between operations  14 us (2%)
    reduce_scatter x1, waiting for transfers between devices, body(): owned = lax.psum_scatter(seq_total, 'dp', scatter_dimension=0, tiled=True)  205 us
    all_gather x1, waiting for transfers between devices, body(): seq_total = jnp.sum(lax.all_gather(local_grad, 'seq'), axis=0)  176 us
    all_gather x2, waiting for transfers between devices, carried_in(): pieces = lax.all_gather(value, axis)  167 us
    select_n x30, other arithmetic, lap(): return jnp.where(position < mine, longer, running)  48 us
  transfers between devices with their start and end apart: 4, of which 4 were waited for; matrix products, arithmetic and copies ran while one was open for 7% of the time, Pallas kernels for 0%

profile of v1, /device:TPU:1, one launch (start us, length us, event | category | flops | bytes accessed | tf_op | source)
XLA Modules:
  0.0 671.6 jit_solution(12270209045013626273)
XLA Ops:
  18.8 2.4 fusion.5
  21.1 96.6 %all-gather.8.cloned.1.call-done = f32[256,128,128]{2,1,0:T(8,128)} async-done(((f32[16,128,128]{2,1,0:T(8,128)}), f32[256,128,128]{2,1,0:T(8,128)}) %all-gather.8.cloned.1.call-update) | async-done | bytes 16777232 | tf_op jit(solution)/shard_map/all_gather | solution.py:10
  117.7 24.4 %while.28 = (s32[]{:T(128)}, f32[16,128,128]{2,1,0:T(8,128)S(1)}, s32[]{:T(128)}, f32[16,16,128,128]{3,2,1,0:T(8,128)}, s32[]{:T(128)}, /*index=5*/s32[]{:T(128)}) while((s32[]{:T(128)}, f32[16,128,128]{2,1,0:T(8,128)S(1)}, s32[]{:T(128)}, f32[16,16,128,128]{3,2,1,0:T(8,128)}, s32[]{:T(128)}, /*index=5*/s32[]{:T(128)}) %tuple.79), condition=%wide.region_1.2_spmd.clone, body=%wide.region_0.1_spmd.clone.sunk | while | flops 786436 | bytes 3145821 | solution.py:20
  119.3 1.6 add_select_fusion.4
  121.0 1.6 add_select_fusion.4
  122.6 1.6 add_select_fusion.4
  125.8 1.6 add_select_fusion.4
  129.0 1.6 add_select_fusion.4
  130.6 1.7 add_select_fusion.4
  134.0 1.6 add_select_fusion.4
  137.2 1.6 add_select_fusion.4
  138.8 1.7 add_select_fusion.4
  140.6 1.6 add_select_fusion.4
  144.0 2.5 convolution_bitcast_fusion.2
  146.5 70.1 %all-gather.10.cloned.1.call-done = f32[256,128,128]{2,1,0:T(8,128)} async-done(((f32[16,128,128]{2,1,0:T(8,128)}), f32[256,128,128]{2,1,0:T(8,128)}) %all-gather.10.cloned.1.call-update) | async-done | bytes 16777232 | tf_op jit(solution)/shard_map/all_gather | solution.py:10
  216.7 11.6 %rev.3 = f32[16,16,128,128]{3,2,1,0:T(8,128)} reverse(f32[16,16,128,128]{3,2,1,0:T(8,128)} %bitcast.81), dimensions={0} | reverse | bytes 33554432 | tf_op jit(solution)/shard_map/rev | solution.py:12
  228.3 24.2 %while.29 = (s32[]{:T(128)}, f32[16,128,128]{2,1,0:T(8,128)S(1)}, s32[]{:T(128)}, f32[16,16,128,128]{3,2,1,0:T(8,128)}, s32[]{:T(128)}, /*index=5*/s32[]{:T(128)}) while((s32[]{:T(128)}, f32[16,128,128]{2,1,0:T(8,128)S(1)}, s32[]{:T(128)}, f32[16,16,128,128]{3,2,1,0:T(8,128)}, s32[]{:T(128)}, /*index=5*/s32[]{:T(128)}) %tuple.68), condition=%wide.region_3.4_spmd.clone, body=%wide.region_2.3_spmd.clone.sunk | while | flops 786436 | bytes 3145821 | solution.py:20
  228.3 1.6 add_select_fusion.5
  230.0 1.6 add_select_fusion.5
  233.2 1.6 add_select_fusion.5
  234.8 1.6 add_select_fusion.5
  236.4 1.6 add_select_fusion.5
  241.3 1.6 add_select_fusion.5
  242.9 1.6 add_select_fusion.5
  244.5 1.6 add_select_fusion.5
  249.3 1.6 add_select_fusion.5
  250.9 1.6 add_select_fusion.5
  257.7 2.8 pad_maximum_fusion
  260.6 175.9 %all-gather.6.cloned.1.call-done = f32[16,4096,128]{2,1,0:T(8,128)} async-done(((f32[1,4096,128]{2,1,0:T(8,128)}), f32[16,4096,128]{2,1,0:T(8,128)}) %all-gather.6.cloned.1.call-update) | async-done | bytes 33554448 | tf_op jit(solution)/shard_map/all_gather | solution.py:79
  436.5 13.1 %reduce_sum.9 = f32[4096,128]{1,0:T(8,128)} reduce(f32[16,4096,128]{2,1,0:T(8,128)} %all-gather.6.cloned.1.call-done, f32[]{:T(128)} %constant.58.clone.1), dimensions={0}, to_apply=%region_4.5 | reduce | flops 7864320 | bytes 35651588 | tf_op jit(solution)/shard_map/reduce_sum | solution.py:79
  450.9 1.7 fusion.8
  458.5 205.1 %reduce-scatter.2.cloned.1.call-done = f32[128,128]{1,0:T(8,128)} async-done(((f32[4096,128]{1,0:T(8,128)}), f32[128,128]{1,0:T(8,128)}) %reduce-scatter.2.cloned.1.call-update) | async-done | bytes 65552 | tf_op jit(solution)/shard_map/reduce_scatter | solution.py:80
  (53 shorter events, 43.0 us)
Async XLA Ops:
  7.2 110.6 %all-gather.8.cloned.1.call-start = ((), (), s32[]{:S(2)}) async-start(), calls=%async_computation.3 | async-start | bytes 17825792 | tf_op jit(solution)/shard_map/all_gather | solution.py:10
  8.5 4.3 copy-start.3
  9.9 5.6 copy-start.4
  12.8 203.8 %all-gather.10.cloned.1.call-start = ((), (), s32[]{:S(2)}) async-start(), calls=%async_computation.4 | async-start | bytes 17825792 | tf_op jit(solution)/shard_map/all_gather | solution.py:10
  15.5 3.2 copy-start.5
  17.1 1.6 copy-start
  18.7 417.8 %all-gather.6.cloned.1.call-start = ((), (), s32[]{:S(2)}) async-start(), calls=%async_computation.1 | async-start | bytes 35651584 | tf_op jit(solution)/shard_map/all_gather | solution.py:79
  228.3 25.8 %copy-start.1 = (bf16[128,16,128]{0,2,1:T(8,128)(2,1)S(1)}, bf16[128,16,128]{0,2,1:T(8,128)(2,1)}, u32[]{:S(2)}) copy-start(bf16[128,16,128]{0,2,1:T(8,128)(2,1)} %copy-done) | copy-start | bytes 1572868
  255.4 0.8 copy-start.2
  260.6 403.0 %reduce-scatter.2.cloned.1.call-start = ((), (), s32[]{:S(2)}) async-start(), calls=%async_computation.2 | async-start | bytes 2162688 | tf_op jit(solution)/shard_map/reduce_scatter | solution.py:80
Sparse Core Ops, SparseCore 0:
  12.9 104.7 all-gather.7
  119.8 96.7 all-gather.9
  260.7 175.7 all-gather.5
  449.7 213.8 reduce-scatter.1
